TPU v7x, 128 devices: a whole 4x4x4 slice. The times are simulated.
128 devices in a mesh: exp: 16 (over y, z_hi, core), row: 8 (over z_lo, x).
Axes of the slice: x: 4, y: 4, z: 4 (z_hi: 2, z_lo: 2; z = z_hi * 2 + z_lo), core: 2. Of those that a mesh axis runs over, the one named last changes fastest.
Arguments:
- exposures: bfloat16 [16, 39, 128, 2048], P('exp', None, 'row'), may hold values from -6 to 6
- fake_flux: float32 [16, 39, 16], P('exp'), may hold values from -24 to 24
- fake_rows: int32 [16], replicated, may hold values from 0 to 127
- fake_cols: int32 [16], replicated, may hold values from 0 to 2047
- kernel_taps: float32 [39, 16], replicated, may hold values from -0.25 to 0.5
- band_offsets: int32 [39], replicated, may hold values from -12 to -4, as said below
- analysis: bfloat16 [8, 39], replicated, may hold values from -1 to 1
- spectral_basis: bfloat16 [39, 8], replicated, may hold values from -2 to 2
- exposure_weights: float32 [16], replicated, may hold values from -4 to 4
Outputs:
- detection_map: float32 [39, 128, 2048], P(None, 'exp', 'row')
Inputs may be any that keep to these rules, and one draw needn't show every extreme that they name: `band_offsets`: each channel's offset lies in a range such that every output pixel reads pixels at most 12 away; some channel has the smallest offset and some the largest.
All inputs are finite; a program needn't handle non-finite values.
Results may differ from a plain program's by a relative error of at most 0.0065.
Values may be sent and summed in bfloat16 or wider, within the bound.
No kernel may reach another device: no remote copies, remote signals or barrier semaphores. Data moves between devices by JAX's collectives and lax.ppermute only.
A program may use at most 128 MiB of HBM per device.

v0:
```python
import jax
import jax.numpy as jnp
from jax import lax
from jax.sharding import PartitionSpec as P

REACH = 12


def band(tap_values, offsets, count_out, count_in, lead):
    outer = lax.broadcasted_iota(jnp.int32, (count_out, count_in), 0)
    inner = lax.broadcasted_iota(jnp.int32, (count_out, count_in), 1)
    distance = inner[None, :, :] - lead - outer[None, :, :] - offsets[:, None, None]
    matrix = jnp.zeros((tap_values.shape[0], count_out, count_in), jnp.float32)
    for tap_index in range(tap_values.shape[1]):
        weight = tap_values[:, tap_index].astype(jnp.float32)[:, None, None]
        matrix = matrix + jnp.where(distance == tap_index, weight, 0.0)
    return matrix.astype(jnp.bfloat16)


def project(resampled, analysis, spectral_basis):
    coefficients = jnp.einsum(
        "kc,echw->ekhw", analysis, resampled, preferred_element_type=jnp.float32
    ).astype(jnp.bfloat16)
    model = jnp.einsum(
        "ck,ekhw->echw", spectral_basis, coefficients, preferred_element_type=jnp.float32
    )
    return (resampled.astype(jnp.float32) - model).astype(jnp.bfloat16)


def body(
    exposures,
    fake_flux,
    fake_rows,
    fake_cols,
    kernel_taps,
    band_offsets,
    analysis,
    spectral_basis,
    exposure_weights,
):
    local_exp, channels, local_rows, width = exposures.shape
    tap_values = kernel_taps.astype(jnp.bfloat16)
    row_start = lax.axis_index("row") * local_rows
    row_ids = row_start + lax.broadcasted_iota(jnp.int32, (local_rows,), 0)
    col_ids = lax.broadcasted_iota(jnp.int32, (width,), 0)
    row_hits = (fake_rows[:, None] == row_ids[None, :]).astype(jnp.float32)
    col_hits = (fake_cols[:, None] == col_ids[None, :]).astype(jnp.float32)
    added = jnp.einsum(
        "ecf,fh,fw->echw", fake_flux, row_hits, col_hits, precision=lax.Precision.HIGHEST
    )
    injected = (exposures.astype(jnp.float32) + added).astype(jnp.bfloat16)
    block = min(512, width)
    column_kernel = band(tap_values, band_offsets, block, block + 2 * REACH, REACH)
    padded = jnp.pad(injected, ((0, 0), (0, 0), (0, 0), (REACH, REACH)))
    pieces = []
    for block_index in range(width // block):
        window = padded[:, :, :, block_index * block : block_index * block + block + 2 * REACH]
        pieces.append(
            jnp.einsum("echj,cwj->echw", window, column_kernel, preferred_element_type=jnp.float32)
        )
    first = jnp.concatenate(pieces, axis=3).astype(jnp.bfloat16)
    columns = lax.all_to_all(first, "row", split_axis=3, concat_axis=2, tiled=True)
    all_rows = columns.shape[2]
    row_kernel = band(tap_values, band_offsets, all_rows, all_rows, 0)
    second = jnp.einsum(
        "cij,ecjw->eciw", row_kernel, columns, preferred_element_type=jnp.float32
    ).astype(jnp.bfloat16)
    residual = project(second, analysis, spectral_basis)
    total_exp = local_exp * lax.axis_size("exp")
    own_weights = lax.dynamic_slice_in_dim(
        exposure_weights, lax.axis_index("exp") * local_exp, local_exp
    )
    values = residual.astype(jnp.float32)
    first_sum = jnp.sum(values, axis=0)
    weighted_sum = jnp.einsum("e,echw->chw", own_weights, values, precision=lax.Precision.HIGHEST)
    square_sum = jnp.sum(values * values, axis=0)
    first_sum, weighted_sum, square_sum = (
        lax.psum_scatter(first_sum, "exp", scatter_dimension=1, tiled=True),
        lax.psum_scatter(weighted_sum, "exp", scatter_dimension=1, tiled=True),
        lax.psum_scatter(square_sum, "exp", scatter_dimension=1, tiled=True),
    )
    mean_level = first_sum / total_exp
    weighted = weighted_sum - mean_level * jnp.sum(exposure_weights)
    spread = square_sum / total_exp - mean_level * mean_level + 1e-05
    return weighted / jnp.sqrt(total_exp * spread)


def solution(mesh):
    return jax.shard_map(
        body,
        mesh=mesh,
        in_specs=(
            P("exp", None, "row", None),
            P("exp", None, None),
            P(),
            P(),
            P(),
            P(),
            P(),
            P(),
            P(),
        ),
        out_specs=P(None, "exp", "row"),
        check_vma=False,
    )
```

profile of v0, /device:TPU:0, one launch (start us, length us, event | category | flops | bytes accessed | tf_op | source)
XLA Modules:
  0.0 530.4 jit_solution(3733225027252749693)
XLA Ops:
  6.7 0.7 convert_element_type.229
  7.4 0.7 compare_convert_fusion
  8.1 6.5 %fusion = bf16[1,39,16,2048]{3,1,2,0:T(8,128)(2,1)S(1)} fusion(bf16[1,39,16,2048]{3,2,1,0:T(8,128)(2,1)} %param.9, s32[16]{0:T(128)} %param.12, f32[16,39]{1,0:T(8,128)} %bitcast.168, f32[16,16]{0,1:T(8,128)S(1)} %compare_convert_fusion), kind=kOutput, calls=%fused_computation.37 | convolution fusion | flops 249243392 | bytes 5115392 | tf_op jit(solution)/shard_map/ecf,fh,fw->echw/dot_general | solution.py:48
  14.6 1.7 fusion.45
  16.3 70.8 %add_convert_fusion = bf16[39,512,536]{1,2,0:T(8,128)(2,1)} fusion(f32[39]{0:T(128)S(1)} %get-tuple-element.12, f32[39]{0:T(128)S(1)} %get-tuple-element.13, f32[39]{0:T(128)S(1)} %get-tuple-element.14, f32[39]{0:T(128)S(1)} %get-tuple-element.15, f32[39]{0:T(128)S(1)} %get-tuple-element.16, f32[39]{0:T(128)S(1)} %get-tuple-element.17, ...), kind=kLoop, calls=%fused_computation.16 | loop fusion | flops 524439552 | bytes 22506076 | tf_op jit(solution)/shard_map/convert_element_type | solution.py:17
  87.1 8.7 %fusion.42 = bf16[1,39,16,512]{3,2,1,0:T(8,128)(2,1)S(1)} fusion(bf16[39,512,536]{1,2,0:T(8,128)(2,1)} %add_convert_fusion, bf16[39,16,536]{2,0,1:T(8,128)(2,1)S(1)} %get-tuple-element.8), kind=kOutput, calls=%fused_computation.90 | convolution fusion | flops 342810624 | bytes 22713600 | tf_op jit(solution)/shard_map/echj,cwj->echw/dot_general | solution.py:59
  95.8 8.9 %fusion.41 = bf16[1,39,16,512]{3,2,1,0:T(8,128)(2,1)S(1)} fusion(bf16[39,512,536]{1,2,0:T(8,128)(2,1)} %add_convert_fusion, bf16[39,16,536]{2,0,1:T(8,128)(2,1)S(1)} %get-tuple-element.9), kind=kOutput, calls=%fused_computation.89 | convolution fusion | flops 342810624 | bytes 22713600 | tf_op jit(solution)/shard_map/echj,cwj->echw/dot_general | solution.py:59
  104.7 8.7 %fusion.40 = bf16[1,39,16,512]{3,2,1,0:T(8,128)(2,1)S(1)} fusion(bf16[39,512,536]{1,2,0:T(8,128)(2,1)} %add_convert_fusion, bf16[39,16,536]{2,0,1:T(8,128)(2,1)S(1)} %get-tuple-element.10), kind=kOutput, calls=%fused_computation.88 | convolution fusion | flops 342810624 | bytes 22713600 | tf_op jit(solution)/shard_map/echj,cwj->echw/dot_general | solution.py:59
  113.4 8.7 %fusion.39 = bf16[1,39,16,512]{3,2,1,0:T(8,128)(2,1)S(1)} fusion(bf16[39,512,536]{1,2,0:T(8,128)(2,1)} %add_convert_fusion, bf16[39,16,536]{2,0,1:T(8,128)(2,1)S(1)} %get-tuple-element.7), kind=kOutput, calls=%fused_computation.87 | convolution fusion | flops 342810624 | bytes 22713600 | tf_op jit(solution)/shard_map/echj,cwj->echw/dot_general | solution.py:59
  122.4 10.2 %copy.62 = bf16[1,39,16,2048]{1,2,0,3:T(8,128)(2,1)} copy(bf16[1,39,16,2048]{3,2,1,0:T(8,128)(2,1)S(1)} %pad_maximum_fusion) | data formatting | bytes 5111808 | tf_op jit(solution)/shard_map/concatenate | solution.py:61
  132.6 16.3 %reshape.268 = bf16[8,2,79872]{2,1,0:T(2,128)(2,1)} reshape(bf16[2048,1,16,39]{3,2,1,0:T(8,128)(2,1)} %bitcast.163) | data formatting | bytes 5111808
  149.0 5.9 %all-to-all-start = ((bf16[8,2,79872]{2,1,0:T(2,128)(2,1)}), bf16[8,2,79872]{2,1,0:T(2,128)(2,1)S(1)}, u32[]{:S(2)}, u32[]{:S(2)}) async-start(bf16[8,2,79872]{2,1,0:T(2,128)(2,1)} %reshape.268), calls=%async_computation | async-start | bytes 5111808 | tf_op jit(solution)/shard_map/all_to_all | solution.py:62
  155.5 31.2 %all-to-all-done = bf16[8,2,79872]{2,1,0:T(2,128)(2,1)S(1)} async-done(((bf16[8,2,79872]{2,1,0:T(2,128)(2,1)}), bf16[8,2,79872]{2,1,0:T(2,128)(2,1)S(1)}, u32[]{:S(2)}, u32[]{:S(2)}) %all-to-all-start) | async-done | bytes 2555936 | tf_op jit(solution)/shard_map/all_to_all | solution.py:62
  186.7 24.8 %reshape.269 = bf16[2048,1,16,39]{3,2,1,0:T(8,128)(2,1)} reshape(bf16[8,2,79872]{2,1,0:T(2,128)(2,1)S(1)} %all-to-all-done) | data formatting | bytes 5111808
  211.5 9.8 %copy.73 = bf16[1,39,16,8,256]{4,3,2,1,0:T(8,128)(2,1)S(1)} copy(bf16[1,39,16,8,256]{1,2,4,3,0:T(8,128)(2,1)} %bitcast.164) | data formatting | bytes 5111808 | tf_op jit(solution)/shard_map/all_to_all | solution.py:62
  221.3 0.8 copy.64
  222.1 6.2 %convolution_convert_fusion = bf16[39,256,128]{2,1,0:T(8,128)(2,1)} fusion(bf16[39,128,256]{2,1,0:T(8,128)(2,1)S(1)} %bitcast.167, f32[39]{0:T(128)S(1)} %get-tuple-element.12, f32[39]{0:T(128)S(1)} %get-tuple-element.13, f32[39]{0:T(128)S(1)} %get-tuple-element.14, f32[39]{0:T(128)S(1)} %get-tuple-element.15, f32[39]{0:T(128)S(1)} %get-tuple-element.16, ...), kind=kOutput, calls=%fused_computation.46 | convolution fusion | flops 359743488 | bytes 5179996 | tf_op jit(solution)/shard_map/cij,ecjw->eciw/dot_general | solution.py:65
  228.3 3.8 copy.66
  232.1 3.5 fusion.44
  235.6 6.2 %copy.67 = f32[128,256,39]{0,1,2:T(8,128)} copy(f32[128,256,39]{1,2,0:T(8,128)} %fusion.44) | data formatting | bytes 10223616 | tf_op jit(solution)/shard_map/ck,ekhw->echw/dot_general | solution.py:24
  241.8 7.3 %fusion.1 = (f32[39,128,256]{1,2,0:T(8,128)}, bf16[1,39,128,256]{2,3,1,0:T(8,128)(2,1)S(1)}) fusion(f32[]{:T(128)} %bitcast, f32[128,256,39]{0,1,2:T(8,128)} %copy.67, bf16[39,256,128]{2,1,0:T(8,128)(2,1)} %convolution_convert_fusion), kind=kLoop, calls=%fused_computation.38 | loop fusion | flops 6389760 | bytes 15335428 | tf_op jit(solution)/shard_map/e,echw->chw/dot_general | solution.py:75
  249.1 6.1 %copy.68 = f32[39,128,256]{2,0,1:T(8,128)} copy(f32[39,128,256]{1,2,0:T(8,128)} %get-tuple-element.5) | data formatting | bytes 10223616 | tf_op jit(solution)/shard_map/e,echw->chw/dot_general | solution.py:75
  255.3 3.0 fusion.2
  258.3 6.1 %copy.70 = f32[39,128,256]{2,0,1:T(8,128)} copy(f32[39,128,256]{1,2,0:T(8,128)} %fusion.2) | data formatting | bytes 10223616 | tf_op jit(solution)/shard_map/reduce_sum | solution.py:76
  264.5 2.8 convert_bitcast_fusion
  267.3 6.2 %copy.69 = f32[39,128,256]{2,0,1:T(8,128)} copy(f32[39,128,256]{1,2,0:T(8,128)} %convert_bitcast_fusion) | data formatting | bytes 10223616 | tf_op jit(solution)/shard_map/reduce_sum | solution.py:74
  273.6 0.6 reduce_sum.16
  274.8 71.2 %reduce-scatter.4.cloned.1.call-done = f32[39,8,256]{2,0,1:T(8,128)} async-done(((f32[39,128,256]{2,0,1:T(8,128)}), f32[39,8,256]{2,0,1:T(8,128)}) %reduce-scatter.4.cloned.1.call-update) | async-done | bytes 319504 | tf_op jit(solution)/shard_map/reduce_scatter | solution.py:79
  346.0 87.9 %reduce-scatter.8.cloned.1.call-done = f32[39,8,256]{2,0,1:T(8,128)} async-done(((f32[39,128,256]{2,0,1:T(8,128)}), f32[39,8,256]{2,0,1:T(8,128)}) %reduce-scatter.8.cloned.1.call-update) | async-done | bytes 319504 | tf_op jit(solution)/shard_map/reduce_scatter | solution.py:80
  433.9 87.9 %reduce-scatter.6.cloned.1.call-done = f32[39,8,256]{2,0,1:T(8,128)} async-done(((f32[39,128,256]{2,0,1:T(8,128)}), f32[39,8,256]{2,0,1:T(8,128)}) %reduce-scatter.6.cloned.1.call-update) | async-done | bytes 319504 | tf_op jit(solution)/shard_map/reduce_scatter | solution.py:78
  521.8 1.3 rsqrt_multiply_fusion
  523.1 0.8 copy.71
  (20 shorter events, 1.2 us)
Async XLA Ops:
  6.5 225.5 %copy-start = (bf16[39,8]{0,1:T(8,128)(2,1)S(1)}, bf16[39,8]{0,1:T(8,128)(2,1)}, u32[]{:S(2)}) copy-start(bf16[39,8]{0,1:T(8,128)(2,1)} %param.16) | copy-start | bytes 1876
  8.1 8.2 %copy-start.2 = (s32[39]{0:T(128)S(1)}, s32[39]{0:T(128)}, u32[]{:S(2)}) copy-start(s32[39]{0:T(128)} %param.14) | copy-start | bytes 472
  149.0 6.0 %copy-start.3 = (f32[16]{0:T(128)S(1)}, f32[16]{0:T(128)}, u32[]{:S(2)}) copy-start(f32[16]{0:T(128)} %param.17) | copy-start | bytes 196
  149.0 37.7 %all-to-all-start = ((bf16[8,2,79872]{2,1,0:T(2,128)(2,1)}), bf16[8,2,79872]{2,1,0:T(2,128)(2,1)S(1)}, u32[]{:S(2)}, u32[]{:S(2)}) async-start(bf16[8,2,79872]{2,1,0:T(2,128)(2,1)} %reshape.268), calls=%async_computation | async-start | bytes 5111808 | tf_op jit(solution)/shard_map/all_to_all | solution.py:62
  154.9 191.1 %reduce-scatter.4.cloned.1.call-start = ((), (), s32[]{:S(2)}) async-start(), calls=%async_computation.4 | async-start | bytes 5570560 | tf_op jit(solution)/shard_map/reduce_scatter | solution.py:79
  228.3 3.8 copy-start.1
  255.2 178.7 %reduce-scatter.8.cloned.1.call-start = ((), (), s32[]{:S(2)}) async-start(), calls=%async_computation.6 | async-start | bytes 5570560 | tf_op jit(solution)/shard_map/reduce_scatter | solution.py:80
  264.4 257.4 %reduce-scatter.6.cloned.1.call-start = ((), (), s32[]{:S(2)}) async-start(), calls=%async_computation.5 | async-start | bytes 5570560 | tf_op jit(solution)/shard_map/reduce_scatter | solution.py:78
Sparse Core Ops, SparseCore 0:
  255.4 90.5 reduce-scatter.3
  350.1 83.8 reduce-scatter.7
  438.0 83.7 reduce-scatter.5
where the time goes:
time: 531 us; the launch traced here: 530 us
  waiting for transfers between devices  278 us (52%)
  local copies, waits for them, and re-layouts  93.5 us (18%)
  other arithmetic  87.6 us (16%)
  matrix products  51.2 us (10%)
  between operations  13.9 us (3%)
  starting transfers between devices  6.02 us (1%)
    reduce_scatter x1, waiting for transfers between devices, body(): lax.psum_scatter(square_sum, 'exp', scatter_dimension=1, tiled=True)  87.9 us
    reduce_scatter x1, waiting for transfers between devices, body(): lax.psum_scatter(first_sum, 'exp', scatter_dimension=1, tiled=True)  87.9 us
    reduce_scatter x1, waiting for transfers between devices, body(): lax.psum_scatter(weighted_sum, 'exp', scatter_dimension=1, tiled=True)  71.2 us
    convert_element_type x1, other arithmetic, band(): return matrix.astype(jnp.bfloat16)  70.8 us
    unnamed x10, local copies, waits for them, and re-layouts  41.1 us
    dot_general x4, matrix products, body(): jnp.einsum('echj,cwj->echw', window, column_kernel, preferred_element_typ...  35 us
    all_to_all x1, waiting for transfers between devices, body(): lax.all_to_all(first, 'row', split_axis=3, concat_axis=2, tiled=True)  31.2 us
  transfers between devices with their start and end apart: 4, of which 4 were waited for; matrix products, arithmetic and copies ran while one was open for 4% of the time, Pallas kernels for 0%

commit v1 on v0

--- a/solution.py
+++ b/solution.py
@@ -59,7 +59,13 @@
             jnp.einsum("echj,cwj->echw", window, column_kernel, preferred_element_type=jnp.float32)
         )
     first = jnp.concatenate(pieces, axis=3).astype(jnp.bfloat16)
-    columns = lax.all_to_all(first, "row", split_axis=3, concat_axis=2, tiled=True)
+    play_positions = lambda local: jnp.concatenate(
+        lax.all_to_all(
+            jnp.stack(jnp.split(local, lax.axis_size("row"), axis=3), axis=0), "row", 0, 0
+        ),
+        axis=2,
+    )
+    columns = play_positions(first)
     all_rows = columns.shape[2]
     row_kernel = band(tap_values, band_offsets, all_rows, all_rows, 0)
     second = jnp.einsum(

time: 531 us -> 475 us (0.89)
  local copies, waits for them, and re-layouts: 93.5 us -> 37.8 us
    unnamed x10 -> x15, local copies, waits for them, and re-layouts: 41.1 us -> 5.25 us
    all_to_all x2 -> x0, local copies, waits for them, and re-layouts: 10.6 us -> none  [body(): lax.all_to_all(first, 'row', split_axis=3, concat_axis=2, tiled=True)]
    concatenate x1 -> x0, local copies, waits for them, and re-layouts: 10.2 us -> none  [body(): first = jnp.concatenate(pieces, axis=3).astype(jnp.bfloat16)]
where the time goes in v1:
time: 475 us; the launch traced here: 474 us
  waiting for transfers between devices  278 us (59%)
  other arithmetic  87.4 us (18%)
  matrix products  51.2 us (11%)
  local copies, waits for them, and re-layouts  37.8 us (8%)
  between operations  13.9 us (3%)
  starting transfers between devices  6.02 us (1%)
    reduce_scatter x1, waiting for transfers between devices, body(): lax.psum_scatter(first_sum, 'exp', scatter_dimension=1, tiled=True)  87.8 us
    reduce_scatter x1, waiting for transfers between devices, body(): lax.psum_scatter(square_sum, 'exp', scatter_dimension=1, tiled=True)  87.8 us
    reduce_scatter x1, waiting for transfers between devices, body(): lax.psum_scatter(weighted_sum, 'exp', scatter_dimension=1, tiled=True)  71.2 us
    convert_element_type x1, other arithmetic, band(): return matrix.astype(jnp.bfloat16)  70.8 us
    dot_general x4, matrix products, body(): jnp.einsum('echj,cwj->echw', window, column_kernel, preferred_element_typ...  35 us
    all_to_all x1, waiting for transfers between devices, body(): lax.all_to_all(jnp.stack(jnp.split(local, lax.axis_size('row'), axis=3),...  31.2 us
  transfers between devices with their start and end apart: 4, of which 4 were waited for; matrix products, arithmetic and copies ran while one was open for 4% of the time, Pallas kernels for 0%

profile of v1, /device:TPU:0, one launch (start us, length us, event | category | flops | bytes accessed | tf_op | source)
XLA Modules:
  0.0 474.4 jit_solution(12559442116831672581)
XLA Ops:
  8.1 6.5 %fusion = bf16[1,39,16,2048]{3,1,2,0:T(8,128)(2,1)S(1)} fusion(bf16[1,39,16,2048]{3,2,1,0:T(8,128)(2,1)} %param.9, s32[16]{0:T(128)} %param.12, f32[16,39]{1,0:T(8,128)} %bitcast.195, f32[16,16]{0,1:T(8,128)S(1)} %compare_convert_fusion), kind=kOutput, calls=%fused_computation.37 | convolution fusion | flops 249243392 | bytes 5115392 | tf_op jit(solution)/shard_map/ecf,fh,fw->echw/dot_general | solution.py:48
  14.6 1.7 fusion.46
  16.3 70.8 %add_convert_fusion = bf16[39,512,536]{1,2,0:T(8,128)(2,1)} fusion(f32[39]{0:T(128)S(1)} %get-tuple-element.12, f32[39]{0:T(128)S(1)} %get-tuple-element.13, f32[39]{0:T(128)S(1)} %get-tuple-element.14, f32[39]{0:T(128)S(1)} %get-tuple-element.15, f32[39]{0:T(128)S(1)} %get-tuple-element.16, f32[39]{0:T(128)S(1)} %get-tuple-element.17, ...), kind=kLoop, calls=%fused_computation.16 | loop fusion | flops 524439552 | bytes 22506076 | tf_op jit(solution)/shard_map/convert_element_type | solution.py:17
  87.1 8.7 %fusion.42 = bf16[1,39,16,512]{3,2,1,0:T(8,128)(2,1)S(1)} fusion(bf16[39,512,536]{1,2,0:T(8,128)(2,1)} %add_convert_fusion, bf16[39,16,536]{2,0,1:T(8,128)(2,1)S(1)} %get-tuple-element.7), kind=kOutput, calls=%fused_computation.89 | convolution fusion | flops 342810624 | bytes 22713600 | tf_op jit(solution)/shard_map/echj,cwj->echw/dot_general | solution.py:59
  95.8 8.9 %fusion.41 = bf16[1,39,16,512]{3,2,1,0:T(8,128)(2,1)S(1)} fusion(bf16[39,512,536]{1,2,0:T(8,128)(2,1)} %add_convert_fusion, bf16[39,16,536]{2,0,1:T(8,128)(2,1)S(1)} %get-tuple-element.8), kind=kOutput, calls=%fused_computation.88 | convolution fusion | flops 342810624 | bytes 22713600 | tf_op jit(solution)/shard_map/echj,cwj->echw/dot_general | solution.py:59
  104.7 8.7 %fusion.40 = bf16[1,39,16,512]{3,2,1,0:T(8,128)(2,1)S(1)} fusion(bf16[39,512,536]{1,2,0:T(8,128)(2,1)} %add_convert_fusion, bf16[39,16,536]{2,0,1:T(8,128)(2,1)S(1)} %get-tuple-element.9), kind=kOutput, calls=%fused_computation.87 | convolution fusion | flops 342810624 | bytes 22713600 | tf_op jit(solution)/shard_map/echj,cwj->echw/dot_general | solution.py:59
  113.4 8.7 %fusion.39 = bf16[1,39,16,512]{3,2,1,0:T(8,128)(2,1)S(1)} fusion(bf16[39,512,536]{1,2,0:T(8,128)(2,1)} %add_convert_fusion, bf16[39,16,536]{2,0,1:T(8,128)(2,1)S(1)} %get-tuple-element.10), kind=kOutput, calls=%fused_computation.86 | convolution fusion | flops 342810624 | bytes 22713600 | tf_op jit(solution)/shard_map/echj,cwj->echw/dot_general | solution.py:59
  122.1 0.8 fusion.58
  122.9 0.7 fusion.57
  123.7 0.7 fusion.56
  124.4 0.7 fusion.55
  125.1 0.7 fusion.54
  125.9 0.7 fusion.53
  126.6 0.8 fusion.52
  127.4 0.7 fusion.51
  128.1 5.9 %all-to-all-start = ((bf16[8,1,39,16,256]{4,3,2,1,0:T(8,128)(2,1)}), bf16[8,1,39,16,256]{4,3,2,1,0:T(8,128)(2,1)S(1)}, u32[]{:S(2)}, u32[]{:S(2)}) async-start(bf16[8,1,39,16,256]{4,3,2,1,0:T(8,128)(2,1)} %fusion.51), calls=%async_computation | async-start | bytes 5111808 | tf_op jit(solution)/shard_map/all_to_all | solution.py:63
  134.7 31.2 %all-to-all-done = bf16[8,1,39,16,256]{4,3,2,1,0:T(8,128)(2,1)S(1)} async-done(((bf16[8,1,39,16,256]{4,3,2,1,0:T(8,128)(2,1)}), bf16[8,1,39,16,256]{4,3,2,1,0:T(8,128)(2,1)S(1)}, u32[]{:S(2)}, u32[]{:S(2)}) %all-to-all-start) | async-done | bytes 2555936 | tf_op jit(solution)/shard_map/all_to_all | solution.py:63
  166.2 6.2 %convolution_convert_fusion = bf16[39,256,128]{2,1,0:T(8,128)(2,1)} fusion(bf16[39,128,256]{2,1,0:T(8,128)(2,1)S(1)} %bitcast.194, f32[39]{0:T(128)S(1)} %get-tuple-element.12, f32[39]{0:T(128)S(1)} %get-tuple-element.13, f32[39]{0:T(128)S(1)} %get-tuple-element.14, f32[39]{0:T(128)S(1)} %get-tuple-element.15, f32[39]{0:T(128)S(1)} %get-tuple-element.16, ...), kind=kOutput, calls=%fused_computation.45 | convolution fusion | flops 359743488 | bytes 5179996 | tf_op jit(solution)/shard_map/cij,ecjw->eciw/dot_general | solution.py:71
  172.4 3.8 copy.35
  176.2 3.5 fusion.44
  179.6 6.2 %copy.36 = f32[128,256,39]{0,1,2:T(8,128)} copy(f32[128,256,39]{1,2,0:T(8,128)} %fusion.44) | data formatting | bytes 10223616 | tf_op jit(solution)/shard_map/ck,ekhw->echw/dot_general | solution.py:24
  185.9 7.3 %fusion.1 = (f32[39,128,256]{1,2,0:T(8,128)}, bf16[1,39,128,256]{2,3,1,0:T(8,128)(2,1)S(1)}) fusion(f32[]{:T(128)} %bitcast, f32[128,256,39]{0,1,2:T(8,128)} %copy.36, bf16[39,256,128]{2,1,0:T(8,128)(2,1)} %convolution_convert_fusion), kind=kLoop, calls=%fused_computation.38 | loop fusion | flops 6389760 | bytes 15335428 | tf_op jit(solution)/shard_map/e,echw->chw/dot_general | solution.py:81
  193.2 6.1 %copy.37 = f32[39,128,256]{2,0,1:T(8,128)} copy(f32[39,128,256]{1,2,0:T(8,128)} %get-tuple-element.5) | data formatting | bytes 10223616 | tf_op jit(solution)/shard_map/e,echw->chw/dot_general | solution.py:81
  199.4 3.0 fusion.2
  202.3 6.1 %copy.39 = f32[39,128,256]{2,0,1:T(8,128)} copy(f32[39,128,256]{1,2,0:T(8,128)} %fusion.2) | data formatting | bytes 10223616 | tf_op jit(solution)/shard_map/reduce_sum | solution.py:82
  208.6 2.8 convert_bitcast_fusion
  211.4 6.2 %copy.38 = f32[39,128,256]{2,0,1:T(8,128)} copy(f32[39,128,256]{1,2,0:T(8,128)} %convert_bitcast_fusion) | data formatting | bytes 10223616 | tf_op jit(solution)/shard_map/reduce_sum | solution.py:80
  218.9 71.2 %reduce-scatter.4.cloned.1.call-done = f32[39,8,256]{2,0,1:T(8,128)} async-done(((f32[39,128,256]{2,0,1:T(8,128)}), f32[39,8,256]{2,0,1:T(8,128)}) %reduce-scatter.4.cloned.1.call-update) | async-done | bytes 319504 | tf_op jit(solution)/shard_map/reduce_scatter | solution.py:85
  290.1 87.8 %reduce-scatter.8.cloned.1.call-done = f32[39,8,256]{2,0,1:T(8,128)} async-done(((f32[39,128,256]{2,0,1:T(8,128)}), f32[39,8,256]{2,0,1:T(8,128)}) %reduce-scatter.8.cloned.1.call-update) | async-done | bytes 319504 | tf_op jit(solution)/shard_map/reduce_scatter | solution.py:86
  377.9 87.8 %reduce-scatter.6.cloned.1.call-done = f32[39,8,256]{2,0,1:T(8,128)} async-done(((f32[39,128,256]{2,0,1:T(8,128)}), f32[39,8,256]{2,0,1:T(8,128)}) %reduce-scatter.6.cloned.1.call-update) | async-done | bytes 319504 | tf_op jit(solution)/shard_map/reduce_scatter | solution.py:84
  465.8 1.3 rsqrt_multiply_fusion
  467.0 0.8 copy.40
  (23 shorter events, 3.3 us)
Async XLA Ops:
  6.5 169.6 %copy-start = (bf16[39,8]{0,1:T(8,128)(2,1)S(1)}, bf16[39,8]{0,1:T(8,128)(2,1)}, u32[]{:S(2)}) copy-start(bf16[39,8]{0,1:T(8,128)(2,1)} %param.16) | copy-start | bytes 1876
  14.6 1.7 copy-start.2
  128.1 6.0 %copy-start.3 = (f32[16]{0:T(128)S(1)}, f32[16]{0:T(128)}, u32[]{:S(2)}) copy-start(f32[16]{0:T(128)} %param.17) | copy-start | bytes 196
  128.1 37.7 %all-to-all-start = ((bf16[8,1,39,16,256]{4,3,2,1,0:T(8,128)(2,1)}), bf16[8,1,39,16,256]{4,3,2,1,0:T(8,128)(2,1)S(1)}, u32[]{:S(2)}, u32[]{:S(2)}) async-start(bf16[8,1,39,16,256]{4,3,2,1,0:T(8,128)(2,1)} %fusion.51), calls=%async_computation | async-start | bytes 5111808 | tf_op jit(solution)/shard_map/all_to_all | solution.py:63
  134.0 156.1 %reduce-scatter.4.cloned.1.call-start = ((), (), s32[]{:S(2)}) async-start(), calls=%async_computation.4 | async-start | bytes 5570560 | tf_op jit(solution)/shard_map/reduce_scatter | solution.py:85
  172.4 3.8 copy-start.1
  199.3 178.6 %reduce-scatter.8.cloned.1.call-start = ((), (), s32[]{:S(2)}) async-start(), calls=%async_computation.6 | async-start | bytes 5570560 | tf_op jit(solution)/shard_map/reduce_scatter | solution.py:86
  208.5 257.2 %reduce-scatter.6.cloned.1.call-start = ((), (), s32[]{:S(2)}) async-start(), calls=%async_computation.5 | async-start | bytes 5570560 | tf_op jit(solution)/shard_map/reduce_scatter | solution.py:84
Sparse Core Ops, SparseCore 0:
  199.4 90.5 reduce-scatter.3
  294.2 83.7 reduce-scatter.7
  382.0 83.7 reduce-scatter.5
